TPU v7x, 32 devices: a whole 2x2x4 slice. The times are simulated.
32 devices in a mesh: ctx: 4 (over z), head: 8 (over y, x, core).
Axes of the slice: x: 2, y: 2, z: 4, core: 2. Of those that a mesh axis runs over, the one named last changes fastest.
Arguments:
- query_rows: bfloat16 [8192, 4096], P('ctx', 'head'), may hold values from -6 to 6
- key_rows: bfloat16 [8192, 4096], P('ctx', 'head'), may hold values from -6 to 6
- value_rows: bfloat16 [8192, 4096], P('ctx', 'head'), may hold values from -6 to 6
- out_grad: bfloat16 [8192, 4096], P('ctx', 'head'), may hold values from -6 to 6
- hub_blocks: int32 [2], replicated, may hold values from 0 to 63, as said below
- local_lists: int32 [64, 6], replicated, may hold values from -3 to 3
Outputs:
- attended: bfloat16 [8192, 4096], P('ctx', 'head')
- query_gradient: bfloat16 [8192, 4096], P('ctx', 'head')
- key_grad: bfloat16 [8192, 4096], P('ctx', 'head')
- value_grad: bfloat16 [8192, 4096], P('ctx', 'head')
Inputs may be any that keep to these rules, and one draw needn't show every extreme that they name: `hub_blocks`: 2 distinct block numbers.
All inputs are finite; a program needn't handle non-finite values.
Results may differ from a plain program's by a relative error of at most 0.012.
The roundings to bfloat16 on the way count: a program that leaves them out, or rounds other values in their place, can miss the bound.
Values may be sent and summed in bfloat16 or wider, within the bound.
A program may use at most 192 MiB of HBM per device.

v0:
```python
import math

import jax
import jax.numpy as jnp
from jax import lax
from jax.sharding import PartitionSpec as P

DH = 128
BLK = 128
HB = 3
G = 2


def padded_2(cells, sides, width):
    for axis, dim in sides:
        count = lax.axis_size(axis)
        ends = count - 1
        head = lax.slice_in_dim(cells, 0, width, axis=dim)
        tail = lax.slice_in_dim(cells, cells.shape[dim] - width, cells.shape[dim], axis=dim)
        cells = jnp.concatenate(
            [
                lax.ppermute(tail, axis, [(i, (i + 1) % count) for i in range(ends)]),
                cells,
                lax.ppermute(head, axis, [((i + 1) % count, i) for i in range(ends)]),
            ],
            axis=dim,
        )
    return cells


def entry_table(block_lists, positions, first_block, total_blocks, extended):
    global_block = first_block - HB + positions
    query_inside = (global_block >= 0) & (global_block < total_blocks)
    key_spot = positions[:, None] + block_lists
    key_global = global_block[:, None] + block_lists
    living = query_inside[:, None] & (key_global >= 0) & (key_global < total_blocks)
    living = living & (key_spot >= 0) & (key_spot < extended)
    set_count = positions.shape[0]
    hub_spots = jnp.broadcast_to(extended + jnp.arange(G, dtype=jnp.int32)[None, :], (set_count, G))
    entries = jnp.concatenate([jnp.clip(key_spot, 0, extended - 1), hub_spots], axis=1)
    all_living = jnp.concatenate(
        [living, jnp.broadcast_to(query_inside[:, None], (set_count, G))], axis=1
    )
    return (entries, all_living)


def grouped(source):
    return source.reshape((source.shape[0] // 4, 4) + source.shape[1:])


def block_scores(query_group, entries, living, key_store, score_scale):
    gathered = key_store[entries]
    logit_scores = (
        jnp.einsum("bqhd,bekhd->bhqek", query_group, gathered, preferred_element_type=jnp.float32)
        * score_scale
    )
    logit_scores = jnp.where(living[:, None, None, :, None], logit_scores, -1e30)
    return (logit_scores, gathered)


def local(query_rows, key_rows, value_rows, out_grad, hub_blocks, local_lists):
    score_scale = 1.0 / math.sqrt(DH)
    ctx_count = lax.axis_size("ctx")
    position = lax.axis_index("ctx")
    tok_rows, columns = query_rows.shape
    head_count = columns // DH
    blocks_here = tok_rows // BLK
    total_blocks = blocks_here * ctx_count
    extended = blocks_here + 2 * HB
    first_block = position * blocks_here
    padded_lists = jnp.pad(local_lists, ((HB, HB), (0, 0)))
    ext_lists = lax.dynamic_slice_in_dim(padded_lists, first_block, extended, 0)
    positions = jnp.arange(extended, dtype=jnp.int32)
    joined = jnp.concatenate([key_rows, value_rows], axis=1)
    widened = padded_2(joined, (("ctx", 0),), HB * BLK)
    far_keys = widened[:, :columns]
    far_values = widened[:, columns : 2 * columns]
    hub_spot = hub_blocks - first_block
    hub_picks = hub_spot[:, None] == jnp.arange(blocks_here, dtype=jnp.int32)[None, :]
    hub_term = jnp.dot(
        hub_picks.astype(jnp.bfloat16),
        joined.reshape(blocks_here, BLK * 2 * columns),
        preferred_element_type=jnp.float32,
    )
    hub_store = lax.psum(hub_term.astype(jnp.bfloat16), "ctx").reshape(G * BLK, 2 * columns)
    key_store = jnp.concatenate([far_keys, hub_store[:, :columns]], axis=0).reshape(
        extended + G, BLK, head_count, DH
    )
    value_store = jnp.concatenate([far_values, hub_store[:, columns:]], axis=0).reshape(
        extended + G, BLK, head_count, DH
    )
    local_entries, local_living = entry_table(
        ext_lists[HB : HB + blocks_here],
        positions[HB : HB + blocks_here],
        first_block,
        total_blocks,
        extended,
    )
    query_blocks = query_rows.reshape(blocks_here, BLK, head_count, DH)
    grad_blocks = out_grad.reshape(blocks_here, BLK, head_count, DH)

    def forward_group(members):
        query_group, entries, living = members
        logit_scores, gathered = block_scores(query_group, entries, living, key_store, score_scale)
        highest = jnp.max(logit_scores, axis=(3, 4), keepdims=True)
        log_norm = highest + jnp.log(
            jnp.sum(jnp.exp(logit_scores - highest), axis=(3, 4), keepdims=True)
        )
        weights = jnp.exp(logit_scores - log_norm).astype(jnp.bfloat16)
        mixed = jnp.einsum(
            "bhqek,bekhd->bqhd", weights, value_store[entries], preferred_element_type=jnp.float32
        )
        return (mixed.astype(jnp.bfloat16), log_norm[:, :, :, 0, 0])

    mixed, norms = lax.map(
        forward_group, (grouped(query_blocks), grouped(local_entries), grouped(local_living))
    )
    attended = mixed.reshape(tok_rows, columns)
    log_norms = norms.reshape(blocks_here, head_count, BLK)
    offsets = jnp.sum(
        grad_blocks.astype(jnp.float32)
        * attended.reshape(blocks_here, BLK, head_count, DH).astype(jnp.float32),
        axis=3,
    )
    offsets = jnp.transpose(offsets, (0, 2, 1))
    set_norms, set_offsets = (log_norms, offsets)
    set_queries, set_grads = (query_blocks, grad_blocks)
    set_entries, set_living = (local_entries, local_living)
    store_rows = extended + G
    store_ids = jnp.arange(store_rows, dtype=jnp.int32)

    def grad_group(carry, members):
        key_acc, value_acc = carry
        query_group, pushed_rows, norm_group, offset_group, entries, living = members
        logit_scores, gathered = block_scores(query_group, entries, living, key_store, score_scale)
        chances = jnp.exp(logit_scores - norm_group[:, :, :, None, None])
        weights = chances.astype(jnp.bfloat16)
        shifted_entries = jnp.einsum(
            "bqhd,bekhd->bhqek",
            pushed_rows,
            value_store[entries],
            preferred_element_type=jnp.float32,
        )
        decay_slopes = (
            chances * (shifted_entries - offset_group[:, :, :, None, None]) * score_scale
        ).astype(jnp.bfloat16)
        query_part = jnp.einsum(
            "bhqek,bekhd->bqhd", decay_slopes, gathered, preferred_element_type=jnp.float32
        )
        key_part = jnp.einsum(
            "bhqek,bqhd->bekhd", decay_slopes, query_group, preferred_element_type=jnp.float32
        )
        value_part = jnp.einsum(
            "bhqek,bqhd->bekhd", weights, pushed_rows, preferred_element_type=jnp.float32
        )
        spots = (
            ((entries[:, :, None] == store_ids[None, None, :]) & living[:, :, None])
            .astype(jnp.float32)
            .reshape(-1, store_rows)
        )
        key_acc = key_acc + jnp.dot(
            spots.T, key_part.reshape(spots.shape[0], -1), precision=lax.Precision.HIGHEST
        )
        value_acc = value_acc + jnp.dot(
            spots.T, value_part.reshape(spots.shape[0], -1), precision=lax.Precision.HIGHEST
        )
        return ((key_acc, value_acc), query_part)

    empty_acc = jnp.zeros((store_rows, BLK * columns), jnp.float32)
    (key_acc, value_acc), query_parts = lax.scan(
        grad_group,
        (empty_acc, empty_acc),
        (
            grouped(set_queries),
            grouped(set_grads),
            grouped(set_norms),
            grouped(set_offsets),
            grouped(set_entries),
            grouped(set_living),
        ),
    )
    query_gradient = (
        query_parts.reshape(-1, BLK, head_count, DH).reshape(tok_rows, columns).astype(jnp.bfloat16)
    )
    gradients = jnp.concatenate([key_acc, value_acc], axis=1)
    owned_rows = gradients[HB : HB + blocks_here]
    rim_rows = jnp.concatenate([gradients[:HB], gradients[HB + blocks_here : extended]], axis=0)
    returned = padded_2(rim_rows.astype(jnp.bfloat16), (("ctx", 0),), HB).astype(rim_rows.dtype)
    owned_rows = owned_rows.at[:HB].add(returned[:HB])
    owned_rows = owned_rows.at[blocks_here - HB :].add(returned[3 * HB :])
    hub_total = lax.psum(gradients[extended : extended + G], "ctx")
    owned_rows = owned_rows + jnp.dot(
        hub_picks.T.astype(jnp.float32), hub_total, precision=lax.Precision.HIGHEST
    )
    key_grad = owned_rows[:, : BLK * columns].reshape(tok_rows, columns).astype(jnp.bfloat16)
    value_grad = owned_rows[:, BLK * columns :].reshape(tok_rows, columns).astype(jnp.bfloat16)
    return (attended, query_gradient, key_grad, value_grad)


def solution(mesh):
    return jax.shard_map(
        local,
        mesh=mesh,
        in_specs=(P("ctx", "head"), P("ctx", "head"), P("ctx", "head"), P("ctx", "head"), P(), P()),
        out_specs=(P("ctx", "head"), P("ctx", "head"), P("ctx", "head"), P("ctx", "head")),
        check_vma=False,
    )
```

profile of v0, /device:TPU:0, one launch (start us, length us, event | category | flops | bytes accessed | tf_op | source)
XLA Modules:
  0.0 707.2 jit_solution(10489579091226312188)
XLA Ops:
  13.0 5.0 collective-permute-start
  19.3 4.8 reshape.209
  39.4 5.2 copy.53
  44.7 26.4 %all-reduce.4.cloned.1.call-done = bf16[256,1024]{1,0:T(8,128)(2,1)} async-done(((bf16[256,1024]{1,0:T(8,128)(2,1)}), bf16[256,1024]{1,0:T(8,128)(2,1)}) %all-reduce.4.cloned.1.call-update) | async-done | bytes 524304 | tf_op jit(solution)/shard_map/psum | solution.py:85
  72.2 7.4 %pad_maximum_fusion = bf16[2816,1024]{1,0:T(8,128)(2,1)S(1)} fusion(bf16[384,1024]{1,0:T(8,128)(2,1)} %collective-permute-done.1, bf16[2048,1024]{1,0:T(8,128)(2,1)} %copy-done.6, bf16[384,1024]{1,0:T(8,128)(2,1)S(1)} %collective-permute-done), kind=kLoop, calls=%fused_computation.72 | loop fusion | flops 17301504 | bytes 11534336 | tf_op jit(solution)/shard_map/concatenate | solution.py:20
  86.7 5.5 reshape.213
  92.2 99.6 %while.29 = (s32[]{:T(128)}, bf16[4,4,128,4,128]{2,4,3,1,0:T(8,128)(2,1)}, f32[4,4,4,128]{3,2,1,0:T(4,128)S(1)}, s32[4,4,8]{2,1,0:T(4,128)S(1)}, bf16[24,128,4,1...) while((s32[]{:T(128)}, ...), condition=%wide.region_4.5_spmd, body=%wide.region_1.4_spmd.sunk | while | flops 1097071744 | bytes 76616880 | solution.py:115
  92.5 5.8 gather_fusion.1
  98.2 7.6 %gather_fusion = bf16[32,128,4,128]{3,2,1,0:T(4,128)(2,1)} fusion(bf16[24,128,4,128]{3,2,1,0:T(4,128)(2,1)} %get-tuple-element.451, s32[1024]{0:T(1024)S(1)} %pad_clamp_fusion.4), kind=kCustom, calls=%fused_computation.1.clone.1 | custom fusion | bytes 8388736 | tf_op jit(solution)/shard_map/while/body/eval_jaxpr/gather | solution.py:52
  117.3 5.8 gather_fusion.1
  123.1 7.6 %gather_fusion = bf16[32,128,4,128]{3,2,1,0:T(4,128)(2,1)} fusion(bf16[24,128,4,128]{3,2,1,0:T(4,128)(2,1)} %get-tuple-element.451, s32[1024]{0:T(1024)S(1)} %pad_clamp_fusion.4), kind=kCustom, calls=%fused_computation.1.clone.1 | custom fusion | bytes 8388736 | tf_op jit(solution)/shard_map/while/body/eval_jaxpr/gather | solution.py:52
  142.2 5.8 gather_fusion.1
  148.0 7.6 %gather_fusion = bf16[32,128,4,128]{3,2,1,0:T(4,128)(2,1)} fusion(bf16[24,128,4,128]{3,2,1,0:T(4,128)(2,1)} %get-tuple-element.451, s32[1024]{0:T(1024)S(1)} %pad_clamp_fusion.4), kind=kCustom, calls=%fused_computation.1.clone.1 | custom fusion | bytes 8388736 | tf_op jit(solution)/shard_map/while/body/eval_jaxpr/gather | solution.py:52
  167.1 5.8 gather_fusion.1
  172.8 7.6 %gather_fusion = bf16[32,128,4,128]{3,2,1,0:T(4,128)(2,1)} fusion(bf16[24,128,4,128]{3,2,1,0:T(4,128)(2,1)} %get-tuple-element.451, s32[1024]{0:T(1024)S(1)} %pad_clamp_fusion.4), kind=kCustom, calls=%fused_computation.1.clone.1 | custom fusion | bytes 8388736 | tf_op jit(solution)/shard_map/while/body/eval_jaxpr/gather | solution.py:52
  195.5 394.3 %while.30 = (s32[]{:T(128)}, f32[24,65536]{1,0:T(8,128)}, f32[24,65536]{1,0:T(8,128)}, bf16[4,4,128,4,128]{2,4,3,1,0:T(8,128)(2,1)}, s32[4,4,8]{2,1,0:T(4,128)S(...) while((s32[]{:T(128)}, f32[24,65536]{1,0:T(8,128)}, ...), condition=%wide.region_7.8_spmd.clone, body=%wide.region_6.7_spmd.clone.sunk | while | flops 3921678336 | bytes 274790528 | solution.py:170
  198.3 5.8 gather_fusion.3
  204.1 7.6 %gather_fusion.2 = bf16[32,128,4,128]{3,2,1,0:T(4,128)(2,1)} fusion(bf16[24,128,4,128]{3,2,1,0:T(4,128)(2,1)} %get-tuple-element.488, s32[1024]{0:T(1024)S(1)} %pad_clamp_fusion.5), kind=kCustom, calls=%fused_computation.2.clone.clone.1 | custom fusion | bytes 8388736 | tf_op jit(solution)/shard_map/while/body/eval_jaxpr/gather | solution.py:52
  211.7 7.4 %copy.105 = bf16[4,8,128,4,128]{2,4,1,3,0:T(8,128)(2,1)} copy(bf16[4,8,128,4,128]{4,3,2,1,0:T(4,128)(2,1)} %bitcast.185) | data formatting | bytes 8388608 | tf_op jit(solution)/shard_map/while/body/eval_jaxpr/gather | solution.py:52
  228.6 4.5 fusion.115
  233.1 9.9 %copy.107 = f32[4,8,128,4,128]{4,3,2,1,0:T(4,128)} copy(f32[4,8,128,4,128]{2,4,1,3,0:T(8,128)} %fusion.115) | data formatting | bytes 16777216 | tf_op jit(solution)/shard_map/while/body/eval_jaxpr/bhqek,bqhd->bekhd/transpose | solution.py:153
  243.0 9.0 %reshape.295 = f32[32,65536]{1,0:T(8,128)} reshape(f32[4,8,128,4,128]{4,3,2,1,0:T(4,128)} %copy.107) | data formatting | bytes 16777216 | tf_op jit(solution)/shard_map/while/body/eval_jaxpr/reshape | solution.py:165
  252.0 8.3 %convolution_add_fusion.6 = f32[24,65536]{1,0:T(8,128)} fusion(f32[32,65536]{1,0:T(8,128)} %reshape.295, f32[24,65536]{1,0:T(8,128)} %get-tuple-element.469, pred[]{:T(512)S(6)} %compare.14, s32[32]{0:T(128)S(1)} %eq.72, pred[32]{0:T(512)(128)(4,1)S(1)} %and.73), kind=kOutput, calls=%fused_computation.30.clone.1 | convolution fusion | flops 607127040 | bytes 20971680 | tf_op jit(solution)/shard_map/while/body/eval_jaxpr/dot_general | solution.py:164
  260.3 5.6 convolution_bitcast_fusion.3
  265.9 9.9 %copy.106 = f32[4,8,128,4,128]{4,3,2,1,0:T(4,128)} copy(f32[4,8,128,4,128]{2,4,1,3,0:T(8,128)} %convolution_bitcast_fusion.3) | data formatting | bytes 16777216 | tf_op jit(solution)/shard_map/while/body/eval_jaxpr/bhqek,bqhd->bekhd/transpose | solution.py:150
  275.8 9.0 %reshape.294 = f32[32,65536]{1,0:T(8,128)} reshape(f32[4,8,128,4,128]{4,3,2,1,0:T(4,128)} %copy.106) | data formatting | bytes 16777216 | tf_op jit(solution)/shard_map/while/body/eval_jaxpr/reshape | solution.py:162
  284.9 8.0 %convolution_add_fusion.5 = f32[24,65536]{1,0:T(8,128)} fusion(f32[32,65536]{1,0:T(8,128)} %reshape.294, f32[24,65536]{1,0:T(8,128)} %get-tuple-element.468, pred[]{:T(512)S(6)} %compare.14, s32[32]{0:T(128)S(1)} %eq.72, pred[32]{0:T(512)(128)(4,1)S(1)} %and.73), kind=kOutput, calls=%fused_computation.31.clone.1 | convolution fusion | flops 607127040 | bytes 20971680 | tf_op jit(solution)/shard_map/while/body/eval_jaxpr/dot_general | solution.py:161
  295.3 5.8 gather_fusion.3
  301.1 7.6 %gather_fusion.2 = bf16[32,128,4,128]{3,2,1,0:T(4,128)(2,1)} fusion(bf16[24,128,4,128]{3,2,1,0:T(4,128)(2,1)} %get-tuple-element.488, s32[1024]{0:T(1024)S(1)} %pad_clamp_fusion.5), kind=kCustom, calls=%fused_computation.2.clone.clone.1 | custom fusion | bytes 8388736 | tf_op jit(solution)/shard_map/while/body/eval_jaxpr/gather | solution.py:52
  308.7 7.4 %copy.105 = bf16[4,8,128,4,128]{2,4,1,3,0:T(8,128)(2,1)} copy(bf16[4,8,128,4,128]{4,3,2,1,0:T(4,128)(2,1)} %bitcast.185) | data formatting | bytes 8388608 | tf_op jit(solution)/shard_map/while/body/eval_jaxpr/gather | solution.py:52
  330.1 9.9 %copy.107 = f32[4,8,128,4,128]{4,3,2,1,0:T(4,128)} copy(f32[4,8,128,4,128]{2,4,1,3,0:T(8,128)} %fusion.115) | data formatting | bytes 16777216 | tf_op jit(solution)/shard_map/while/body/eval_jaxpr/bhqek,bqhd->bekhd/transpose | solution.py:153
  340.0 9.0 %reshape.295 = f32[32,65536]{1,0:T(8,128)} reshape(f32[4,8,128,4,128]{4,3,2,1,0:T(4,128)} %copy.107) | data formatting | bytes 16777216 | tf_op jit(solution)/shard_map/while/body/eval_jaxpr/reshape | solution.py:165
  349.1 9.2 %convolution_add_fusion.6 = f32[24,65536]{1,0:T(8,128)} fusion(f32[32,65536]{1,0:T(8,128)} %reshape.295, f32[24,65536]{1,0:T(8,128)} %get-tuple-element.469, pred[]{:T(512)S(6)} %compare.14, s32[32]{0:T(128)S(1)} %eq.72, pred[32]{0:T(512)(128)(4,1)S(1)} %and.73), kind=kOutput, calls=%fused_computation.30.clone.1 | convolution fusion | flops 607127040 | bytes 20971680 | tf_op jit(solution)/shard_map/while/body/eval_jaxpr/dot_general | solution.py:164
  358.3 5.6 convolution_bitcast_fusion.3
  363.9 9.9 %copy.106 = f32[4,8,128,4,128]{4,3,2,1,0:T(4,128)} copy(f32[4,8,128,4,128]{2,4,1,3,0:T(8,128)} %convolution_bitcast_fusion.3) | data formatting | bytes 16777216 | tf_op jit(solution)/shard_map/while/body/eval_jaxpr/bhqek,bqhd->bekhd/transpose | solution.py:150
  373.8 9.0 %reshape.294 = f32[32,65536]{1,0:T(8,128)} reshape(f32[4,8,128,4,128]{4,3,2,1,0:T(4,128)} %copy.106) | data formatting | bytes 16777216 | tf_op jit(solution)/shard_map/while/body/eval_jaxpr/reshape | solution.py:162
  382.8 9.0 %convolution_add_fusion.5 = f32[24,65536]{1,0:T(8,128)} fusion(f32[32,65536]{1,0:T(8,128)} %reshape.294, f32[24,65536]{1,0:T(8,128)} %get-tuple-element.468, pred[]{:T(512)S(6)} %compare.14, s32[32]{0:T(128)S(1)} %eq.72, pred[32]{0:T(512)(128)(4,1)S(1)} %and.73), kind=kOutput, calls=%fused_computation.31.clone.1 | convolution fusion | flops 607127040 | bytes 20971680 | tf_op jit(solution)/shard_map/while/body/eval_jaxpr/dot_general | solution.py:161
  394.2 5.7 gather_fusion.3
  400.0 7.6 %gather_fusion.2 = bf16[32,128,4,128]{3,2,1,0:T(4,128)(2,1)} fusion(bf16[24,128,4,128]{3,2,1,0:T(4,128)(2,1)} %get-tuple-element.488, s32[1024]{0:T(1024)S(1)} %pad_clamp_fusion.5), kind=kCustom, calls=%fused_computation.2.clone.clone.1 | custom fusion | bytes 8388736 | tf_op jit(solution)/shard_map/while/body/eval_jaxpr/gather | solution.py:52
  407.6 7.4 %copy.105 = bf16[4,8,128,4,128]{2,4,1,3,0:T(8,128)(2,1)} copy(bf16[4,8,128,4,128]{4,3,2,1,0:T(4,128)(2,1)} %bitcast.185) | data formatting | bytes 8388608 | tf_op jit(solution)/shard_map/while/body/eval_jaxpr/gather | solution.py:52
  429.0 9.9 %copy.107 = f32[4,8,128,4,128]{4,3,2,1,0:T(4,128)} copy(f32[4,8,128,4,128]{2,4,1,3,0:T(8,128)} %fusion.115) | data formatting | bytes 16777216 | tf_op jit(solution)/shard_map/while/body/eval_jaxpr/bhqek,bqhd->bekhd/transpose | solution.py:153
  438.9 9.0 %reshape.295 = f32[32,65536]{1,0:T(8,128)} reshape(f32[4,8,128,4,128]{4,3,2,1,0:T(4,128)} %copy.107) | data formatting | bytes 16777216 | tf_op jit(solution)/shard_map/while/body/eval_jaxpr/reshape | solution.py:165
  447.9 9.2 %convolution_add_fusion.6 = f32[24,65536]{1,0:T(8,128)} fusion(f32[32,65536]{1,0:T(8,128)} %reshape.295, f32[24,65536]{1,0:T(8,128)} %get-tuple-element.469, pred[]{:T(512)S(6)} %compare.14, s32[32]{0:T(128)S(1)} %eq.72, pred[32]{0:T(512)(128)(4,1)S(1)} %and.73), kind=kOutput, calls=%fused_computation.30.clone.1 | convolution fusion | flops 607127040 | bytes 20971680 | tf_op jit(solution)/shard_map/while/body/eval_jaxpr/dot_general | solution.py:164
  457.2 5.6 convolution_bitcast_fusion.3
  462.7 9.9 %copy.106 = f32[4,8,128,4,128]{4,3,2,1,0:T(4,128)} copy(f32[4,8,128,4,128]{2,4,1,3,0:T(8,128)} %convolution_bitcast_fusion.3) | data formatting | bytes 16777216 | tf_op jit(solution)/shard_map/while/body/eval_jaxpr/bhqek,bqhd->bekhd/transpose | solution.py:150
  472.7 9.0 %reshape.294 = f32[32,65536]{1,0:T(8,128)} reshape(f32[4,8,128,4,128]{4,3,2,1,0:T(4,128)} %copy.106) | data formatting | bytes 16777216 | tf_op jit(solution)/shard_map/while/body/eval_jaxpr/reshape | solution.py:162
  481.7 9.0 %convolution_add_fusion.5 = f32[24,65536]{1,0:T(8,128)} fusion(f32[32,65536]{1,0:T(8,128)} %reshape.294, f32[24,65536]{1,0:T(8,128)} %get-tuple-element.468, pred[]{:T(512)S(6)} %compare.14, s32[32]{0:T(128)S(1)} %eq.72, pred[32]{0:T(512)(128)(4,1)S(1)} %and.73), kind=kOutput, calls=%fused_computation.31.clone.1 | convolution fusion | flops 607127040 | bytes 20971680 | tf_op jit(solution)/shard_map/while/body/eval_jaxpr/dot_general | solution.py:161
  493.1 5.8 gather_fusion.3
  498.9 7.6 %gather_fusion.2 = bf16[32,128,4,128]{3,2,1,0:T(4,128)(2,1)} fusion(bf16[24,128,4,128]{3,2,1,0:T(4,128)(2,1)} %get-tuple-element.488, s32[1024]{0:T(1024)S(1)} %pad_clamp_fusion.5), kind=kCustom, calls=%fused_computation.2.clone.clone.1 | custom fusion | bytes 8388736 | tf_op jit(solution)/shard_map/while/body/eval_jaxpr/gather | solution.py:52
  506.5 7.4 %copy.105 = bf16[4,8,128,4,128]{2,4,1,3,0:T(8,128)(2,1)} copy(bf16[4,8,128,4,128]{4,3,2,1,0:T(4,128)(2,1)} %bitcast.185) | data formatting | bytes 8388608 | tf_op jit(solution)/shard_map/while/body/eval_jaxpr/gather | solution.py:52
  527.9 9.9 %copy.107 = f32[4,8,128,4,128]{4,3,2,1,0:T(4,128)} copy(f32[4,8,128,4,128]{2,4,1,3,0:T(8,128)} %fusion.115) | data formatting | bytes 16777216 | tf_op jit(solution)/shard_map/while/body/eval_jaxpr/bhqek,bqhd->bekhd/transpose | solution.py:153
  537.8 9.0 %reshape.295 = f32[32,65536]{1,0:T(8,128)} reshape(f32[4,8,128,4,128]{4,3,2,1,0:T(4,128)} %copy.107) | data formatting | bytes 16777216 | tf_op jit(solution)/shard_map/while/body/eval_jaxpr/reshape | solution.py:165
  546.9 9.2 %convolution_add_fusion.6 = f32[24,65536]{1,0:T(8,128)} fusion(f32[32,65536]{1,0:T(8,128)} %reshape.295, f32[24,65536]{1,0:T(8,128)} %get-tuple-element.469, pred[]{:T(512)S(6)} %compare.14, s32[32]{0:T(128)S(1)} %eq.72, pred[32]{0:T(512)(128)(4,1)S(1)} %and.73), kind=kOutput, calls=%fused_computation.30.clone.1 | convolution fusion | flops 607127040 | bytes 20971680 | tf_op jit(solution)/shard_map/while/body/eval_jaxpr/dot_general | solution.py:164
  556.1 5.6 convolution_bitcast_fusion.3
  561.7 9.9 %copy.106 = f32[4,8,128,4,128]{4,3,2,1,0:T(4,128)} copy(f32[4,8,128,4,128]{2,4,1,3,0:T(8,128)} %convolution_bitcast_fusion.3) | data formatting | bytes 16777216 | tf_op jit(solution)/shard_map/while/body/eval_jaxpr/bhqek,bqhd->bekhd/transpose | solution.py:150
  571.6 9.0 %reshape.294 = f32[32,65536]{1,0:T(8,128)} reshape(f32[4,8,128,4,128]{4,3,2,1,0:T(4,128)} %copy.106) | data formatting | bytes 16777216 | tf_op jit(solution)/shard_map/while/body/eval_jaxpr/reshape | solution.py:162
  580.6 9.0 %convolution_add_fusion.5 = f32[24,65536]{1,0:T(8,128)} fusion(f32[32,65536]{1,0:T(8,128)} %reshape.294, f32[24,65536]{1,0:T(8,128)} %get-tuple-element.468, pred[]{:T(512)S(6)} %compare.14, s32[32]{0:T(128)S(1)} %eq.72, pred[32]{0:T(512)(128)(4,1)S(1)} %and.73), kind=kOutput, calls=%fused_computation.31.clone.1 | convolution fusion | flops 607127040 | bytes 20971680 | tf_op jit(solution)/shard_map/while/body/eval_jaxpr/dot_general | solution.py:161
  589.8 6.1 constant_dynamic-update-slice_fusion.3
  598.9 5.2 convert.12
  617.9 8.4 %slice.127 = f32[16,131072]{1,0:T(8,128)} slice(f32[24,131072]{1,0:T(8,128)} %constant_dynamic-update-slice_fusion.2), slice={[3:19], [0:131072]} | slice | bytes 16777216 | tf_op jit(solution)/shard_map/slice | solution.py:186
  638.9 20.5 %scatter-add.6 = f32[16,131072]{1,0:T(8,128)} dynamic-update-slice(f32[16,131072]{1,0:T(8,128)} %slice.127, f32[3,131072]{1,0:T(4,128)S(1)} %convert_add_fusion, s32[]{:T(128)} %constant.122.clone.1, s32[]{:T(128)} %constant.122.clone.1) | dynamic-update-slice | bytes 3145732 | tf_op jit(solution)/shard_map/scatter-add | solution.py:189
  663.6 13.4 %scatter-add.9 = f32[16,131072]{1,0:T(8,128)} dynamic-update-slice(f32[16,131072]{1,0:T(8,128)} %scatter-add.6, f32[3,131072]{1,0:T(4,128)S(1)} %slice_add_fusion, s32[]{:T(128)} %constant.132.clone.1, s32[]{:T(128)} %constant.122.clone.1) | dynamic-update-slice | bytes 3145732 | tf_op jit(solution)/shard_map/scatter-add | solution.py:190
  677.0 9.6 %all-reduce.6.cloned.1.call-done = f32[2,131072]{1,0:T(2,128)} async-done(((f32[2,131072]{1,0:T(2,128)}), f32[2,131072]{1,0:T(2,128)}) %all-reduce.6.cloned.1.call-update) | async-done | bytes 1048592 | tf_op jit(solution)/shard_map/psum | solution.py:191
  686.6 6.9 fusion.58
  (210 shorter events, 180.7 us)
Async XLA Ops:
  7.2 2.2 copy-start.8
  7.2 63.9 %all-reduce.4.cloned.1.call-start = ((), (), s32[]{:S(2)}) async-start(), calls=%async_computation | async-start | bytes 1048576 | tf_op jit(solution)/shard_map/psum | solution.py:85
  9.7 2.0 copy-start.6
  13.0 59.1 %collective-permute-start = (bf16[384,1024]{1,0:T(8,128)(2,1)}, bf16[384,1024]{1,0:T(8,128)(2,1)S(1)}, u32[]{:S(2)}, u32[]{:S(2)}) collective-permute-start(bf16[384,1024]{1,0:T(8,128)(2,1)} %get-tuple-element.282), channel_id=1, source_target_pairs={{0,8},{8,16},{16,24},{1,9},{9,17},{17,25},{2,10},{10,18},{18,26},{... | collective-permute-start | bytes 2359304 | tf_op jit(solution)/shard_map/ppermute | solution.py:22
  18.0 54.1 %collective-permute-start.1 = (bf16[384,1024]{1,0:T(8,128)(2,1)}, bf16[384,1024]{1,0:T(8,128)(2,1)}, u32[]{:S(2)}, u32[]{:S(2)}) collective-permute-start(bf16[384,1024]{1,0:T(8,128)(2,1)} %get-tuple-element.283), channel_id=1, source_target_pairs={{8,0},{16,8},{24,16},{9,1},{17,9},{25,17},{10,2},{18,10},{26,18},{... | collective-permute-start | bytes 2359304 | tf_op jit(solution)/shard_map/ppermute | solution.py:24
  19.3 4.8 copy-start.12
  24.1 5.0 copy-start.7
  24.1 0.5 copy-start.10
  29.1 657.5 %all-reduce.6.cloned.1.call-start = ((), (), s32[]{:S(2)}) async-start(), calls=%async_computation.1 | async-start | bytes 2097152 | tf_op jit(solution)/shard_map/psum | solution.py:191
  31.2 3.3 copy-start.9
  111.5 2.2 copy-start.3
  136.4 2.2 copy-start.3
  161.2 2.2 copy-start.3
  186.1 2.2 copy-start.3
  219.1 3.7 copy-start.4
  219.1 3.8 copy-start.5
  222.9 3.5 copy-start
  226.4 2.2 copy-start.1
  252.0 8.3 %copy-start.2 = (bf16[4,4,128,8,128]{4,2,3,1,0:T(8,128)(2,1)S(1)}, bf16[4,4,128,8,128]{4,2,3,1,0:T(8,128)(2,1)}, u32[]{:S(2)}) copy-start(bf16[4,4,128,8,128]{4,2,3,1,0:T(8,128)(2,1)} %copy-done.1) | copy-start | bytes 12582916 | tf_op jit(solution)/shard_map/while
  316.1 3.7 copy-start.4
  316.1 3.8 copy-start.5
  319.9 3.5 copy-start
  323.4 2.2 copy-start.1
  349.0 9.2 %copy-start.2 = (bf16[4,4,128,8,128]{4,2,3,1,0:T(8,128)(2,1)S(1)}, bf16[4,4,128,8,128]{4,2,3,1,0:T(8,128)(2,1)}, u32[]{:S(2)}) copy-start(bf16[4,4,128,8,128]{4,2,3,1,0:T(8,128)(2,1)} %copy-done.1) | copy-start | bytes 12582916 | tf_op jit(solution)/shard_map/while
  415.0 3.7 copy-start.4
  415.0 3.8 copy-start.5
  418.8 3.5 copy-start
  422.3 2.2 copy-start.1
  447.9 9.2 %copy-start.2 = (bf16[4,4,128,8,128]{4,2,3,1,0:T(8,128)(2,1)S(1)}, bf16[4,4,128,8,128]{4,2,3,1,0:T(8,128)(2,1)}, u32[]{:S(2)}) copy-start(bf16[4,4,128,8,128]{4,2,3,1,0:T(8,128)(2,1)} %copy-done.1) | copy-start | bytes 12582916 | tf_op jit(solution)/shard_map/while
  513.9 3.7 copy-start.4
  513.9 3.8 copy-start.5
  517.7 3.5 copy-start
  521.2 2.2 copy-start.1
  546.9 9.2 %copy-start.2 = (bf16[4,4,128,8,128]{4,2,3,1,0:T(8,128)(2,1)S(1)}, bf16[4,4,128,8,128]{4,2,3,1,0:T(8,128)(2,1)}, u32[]{:S(2)}) copy-start(bf16[4,4,128,8,128]{4,2,3,1,0:T(8,128)(2,1)} %copy-done.1) | copy-start | bytes 12582916 | tf_op jit(solution)/shard_map/while
  589.8 6.1 slice-start
  589.8 6.1 slice-start.1
  606.3 26.5 %collective-permute-start.2 = (bf16[3,131072]{1,0:T(4,128)(2,1)}, bf16[3,131072]{1,0:T(4,128)(2,1)S(1)}, u32[]{:S(2)}, u32[]{:S(2)}) collective-permute-start(bf16[3,131072]{1,0:T(4,128)(2,1)} %get-tuple-element.276), channel_id=1, source_target_pairs={{0,8},{8,16},{16,24},{1,9},{9,17},{17,25},{2,10},{10,18},{18,26},{... | collective-permute-start | bytes 2359304 | tf_op jit(solution)/shard_map/ppermute | solution.py:22
  609.9 24.7 %collective-permute-start.3 = (bf16[3,131072]{1,0:T(4,128)(2,1)}, bf16[3,131072]{1,0:T(4,128)(2,1)}, u32[]{:S(2)}, u32[]{:S(2)}) collective-permute-start(bf16[3,131072]{1,0:T(4,128)(2,1)} %get-tuple-element.277), channel_id=1, source_target_pairs={{8,0},{16,8},{24,16},{9,1},{17,9},{25,17},{10,2},{18,10},{26,18},{... | collective-permute-start | bytes 2359304 | tf_op jit(solution)/shard_map/ppermute | solution.py:24
  663.6 23.0 %copy-start.11 = (s32[2]{0:T(128)S(1)}, s32[2]{0:T(128)}, u32[]{:S(2)}) copy-start(s32[2]{0:T(128)} %copy-done.10) | copy-start | bytes 28
Sparse Core Ops, SparseCore 0:
  29.2 41.8 all-reduce.3
  632.9 53.6 all-reduce.5
where the time goes:
time: 718 us; the launch traced here: 707 us
  local copies, waits for them, and re-layouts  424 us (59%)
  matrix products  183 us (25%)
  waiting for transfers between devices  37.9 us (5%)
  other arithmetic  35.4 us (5%)
  between operations  14.5 us (2%)
  starting transfers between devices  11.3 us (2%)
    gather x16, local copies, waits for them, and re-layouts, block_scores(): gathered = key_store[entries]  104 us
    transpose x4, local copies, waits for them, and re-layouts, grad_group(): jnp.einsum('bhqek,bqhd->bekhd', weights, pushed_rows, preferred_element_t...  39.6 us
    transpose x4, local copies, waits for them, and re-layouts, grad_group(): jnp.einsum('bhqek,bqhd->bekhd', decay_slopes, query_group, preferred_elem...  39.6 us
    reshape x4, local copies, waits for them, and re-layouts, grad_group(): value_part.reshape(spots.shape[0], -1)  36.2 us
    reshape x4, local copies, waits for them, and re-layouts, grad_group(): key_part.reshape(spots.shape[0], -1)  36.2 us
    dot_general x4, matrix products, grad_group(): jnp.dot(spots.T, value_part.reshape(spots.shape[0], -1), precision=lax.Pr...  35.9 us
    dot_general x4, matrix products, grad_group(): jnp.dot(spots.T, key_part.reshape(spots.shape[0], -1), precision=lax.Prec...  35.1 us
    psum x1, waiting for transfers between devices, local(): lax.psum(hub_term.astype(jnp.bfloat16), 'ctx').reshape(G * BLK, 2 * columns)  26.4 us
  transfers between devices with their start and end apart: 6, of which 3 were waited for; matrix products, arithmetic and copies ran while one was open for 13% of the time, Pallas kernels for 0%

commit v1 on v0

v1 whole, which is shorter than its diff:
```python
import functools
import math

import jax
import jax.numpy as jnp
from jax import lax
from jax.experimental import pallas as pl
from jax.experimental.pallas import tpu as pltpu
from jax.sharding import PartitionSpec as P

DH = 128
BLK = 128
HB = 3
G = 2
DEAD = -1e30


def attend_kernel(
    total_blocks,
    listed,
    width,
    lists_ref,
    q_ref,
    k_ref,
    v_ref,
    g_ref,
    left_ref,
    right_ref,
    hub_ref,
    att_ref,
    dq_ref,
    dk_ref,
    dv_ref,
    dleft_ref,
    dright_ref,
    dhub_ref,
    kx,
    vx,
    kt,
    vt,
    dka,
    dva,
):
    blocks = q_ref.shape[0]
    extended = blocks + 2 * HB
    store = extended + G
    heads = width // DH
    scale = 1.0 / math.sqrt(DH)
    c = scale * math.log2(math.e)
    first_block = lax.axis_index("ctx") * blocks

    kx[0:HB] = left_ref[0]
    vx[0:HB] = left_ref[1]
    kx[HB : HB + blocks] = k_ref[...]
    vx[HB : HB + blocks] = v_ref[...]
    kx[HB + blocks : extended] = right_ref[0]
    vx[HB + blocks : extended] = right_ref[1]
    kx[extended:store] = hub_ref[0]
    vx[extended:store] = hub_ref[1]

    def flip(i, carry):
        for h in range(heads):
            hs = slice(h * DH, (h + 1) * DH)
            kt[i, h] = kx[i, :, hs].T
            vt[i, h] = vx[i, :, hs].T
            dka[i, h] = jnp.zeros((BLK, DH), jnp.float32)
            dva[i, h] = jnp.zeros((BLK, DH), jnp.float32)
        return carry

    lax.fori_loop(0, store, flip, 0)

    def body(b, carry):
        spots = []
        bias = []
        for j in range(listed):
            offset = lists_ref[first_block + b, j]
            there = first_block + b + offset
            alive = (there >= 0) & (there < total_blocks)
            spots.append(HB + b + offset)
            bias.append(jnp.where(alive, 0.0, DEAD))
        for j in range(G):
            spots.append(extended + j)
            bias.append(0.0)
        n = len(spots)
        for h in range(heads):
            hs = slice(h * DH, (h + 1) * DH)
            q = q_ref[b, :, hs]
            g = g_ref[b, :, hs]
            qt = q.T
            gt = g.T
            keys = jnp.concatenate([kx[i, :, hs] for i in spots], axis=0)
            s = jnp.dot(keys, qt, preferred_element_type=jnp.float32)
            parts = [s[e * BLK : (e + 1) * BLK] for e in range(n)]
            tops = [jnp.max(parts[e], axis=0, keepdims=True) * c + bias[e] for e in range(n)]
            top = functools.reduce(jnp.maximum, tops)
            ps = [jnp.exp2(parts[e] * c + (bias[e] - top)) for e in range(n)]
            total = functools.reduce(
                jnp.add, [jnp.sum(p, axis=0, keepdims=True) for p in ps]
            )
            inverse = 1.0 / total
            chances = jnp.concatenate(ps, axis=0) * inverse
            weights = chances.astype(jnp.bfloat16)
            values_t = jnp.concatenate([vt[i, h] for i in spots], axis=1)
            mixed_t = jnp.dot(values_t, weights, preferred_element_type=jnp.float32)
            mixed = mixed_t.T.astype(jnp.bfloat16)
            att_ref[b, :, hs] = mixed
            rounded = mixed_t.astype(jnp.bfloat16).astype(jnp.float32)
            offsets = jnp.sum(gt.astype(jnp.float32) * rounded, axis=0, keepdims=True)
            values = jnp.concatenate([vx[i, :, hs] for i in spots], axis=0)
            pushed = jnp.dot(values, gt, preferred_element_type=jnp.float32)
            slopes = (chances * (pushed - offsets)).astype(jnp.bfloat16)
            keys_t = jnp.concatenate([kt[i, h] for i in spots], axis=1)
            dq_t = jnp.dot(keys_t, slopes, preferred_element_type=jnp.float32) * scale
            dq_ref[b, :, hs] = dq_t.T.astype(jnp.bfloat16)
            dk_part = jnp.dot(slopes, q, preferred_element_type=jnp.float32)
            dv_part = jnp.dot(weights, g, preferred_element_type=jnp.float32)
            for e in range(n):
                dka[spots[e], h] += dk_part[e * BLK : (e + 1) * BLK]
                dva[spots[e], h] += dv_part[e * BLK : (e + 1) * BLK]
        return carry

    lax.fori_loop(0, blocks, body, 0)

    for h in range(heads):
        hs = slice(h * DH, (h + 1) * DH)
        dleft_ref[0, :, :, hs] = (dka[0:HB, h] * scale).astype(jnp.bfloat16)
        dleft_ref[1, :, :, hs] = dva[0:HB, h].astype(jnp.bfloat16)
        dright_ref[0, :, :, hs] = (dka[HB + blocks : extended, h] * scale).astype(jnp.bfloat16)
        dright_ref[1, :, :, hs] = dva[HB + blocks : extended, h].astype(jnp.bfloat16)
        dhub_ref[0, :, :, hs] = (dka[extended:store, h] * scale).astype(dhub_ref.dtype)
        dhub_ref[1, :, :, hs] = dva[extended:store, h].astype(dhub_ref.dtype)

    def finish(i, carry):
        for h in range(heads):
            hs = slice(h * DH, (h + 1) * DH)
            dk_ref[i, :, hs] = (dka[HB + i, h] * scale).astype(jnp.bfloat16)
            dv_ref[i, :, hs] = dva[HB + i, h].astype(jnp.bfloat16)
        return carry

    lax.fori_loop(0, blocks, finish, 0)


def attend(local_lists, q, k, v, g, left, right, hub, total_blocks):
    blocks, _, columns = q.shape
    width = 2 * DH if columns % (2 * DH) == 0 else DH
    heads = width // DH
    store = blocks + 2 * HB + G
    whole = pl.BlockSpec((blocks, BLK, width), lambda i: (0, 0, i))
    rim = pl.BlockSpec((2, HB, BLK, width), lambda i: (0, 0, 0, i))
    hubs = pl.BlockSpec((2, G, BLK, width), lambda i: (0, 0, 0, i))
    big = jax.ShapeDtypeStruct(q.shape, jnp.bfloat16)
    rim_shape = jax.ShapeDtypeStruct(left.shape, jnp.bfloat16)
    hub_shape = jax.ShapeDtypeStruct(hub.shape, jnp.float32)
    return pl.pallas_call(
        functools.partial(attend_kernel, total_blocks, local_lists.shape[1], width),
        grid=(columns // width,),
        in_specs=[pl.BlockSpec(memory_space=pltpu.SMEM)] + [whole] * 4 + [rim, rim, hubs],
        out_specs=[whole] * 4 + [rim, rim, hubs],
        out_shape=[big] * 4 + [rim_shape, rim_shape, hub_shape],
        scratch_shapes=[
            pltpu.VMEM((store, BLK, width), jnp.bfloat16),
            pltpu.VMEM((store, BLK, width), jnp.bfloat16),
            pltpu.VMEM((store, heads, DH, BLK), jnp.bfloat16),
            pltpu.VMEM((store, heads, DH, BLK), jnp.bfloat16),
            pltpu.VMEM((store, heads, BLK, DH), jnp.float32),
            pltpu.VMEM((store, heads, BLK, DH), jnp.float32),
        ],
        compiler_params=pltpu.CompilerParams(vmem_limit_bytes=60 << 20),
        name="attend",
    )(local_lists, q, k, v, g, left, right, hub)


def local(query_rows, key_rows, value_rows, out_grad, hub_blocks, local_lists):
    count = lax.axis_size("ctx")
    tok_rows, columns = query_rows.shape
    blocks = tok_rows // BLK
    total_blocks = blocks * count
    first_block = lax.axis_index("ctx") * blocks
    up = [(i, i + 1) for i in range(count - 1)]
    down = [(i + 1, i) for i in range(count - 1)]
    q, k, v, g = (
        a.reshape(blocks, BLK, columns) for a in (query_rows, key_rows, value_rows, out_grad)
    )
    spots = hub_blocks - first_block
    here = (spots >= 0) & (spots < blocks)
    clipped = jnp.clip(spots, 0, blocks - 1)

    def pick(a):
        rows = [
            jnp.where(here[j], lax.dynamic_index_in_dim(a, clipped[j], 0, keepdims=False), 0)
            for j in range(G)
        ]
        return jnp.stack(rows)

    hub = lax.psum(jnp.stack([pick(k), pick(v)]), "ctx")
    left = lax.ppermute(jnp.stack([k[-HB:], v[-HB:]]), "ctx", up)
    right = lax.ppermute(jnp.stack([k[:HB], v[:HB]]), "ctx", down)
    attended, dq, dk, dv, dleft, dright, dhub = attend(
        local_lists, q, k, v, g, left, right, hub, total_blocks
    )
    from_right = lax.ppermute(dleft, "ctx", down)
    from_left = lax.ppermute(dright, "ctx", up)
    hub_total = lax.psum(dhub, "ctx")
    number = jnp.arange(blocks, dtype=jnp.int32)[:, None, None]

    def finish(own, part):
        middle = jnp.zeros((blocks - 2 * HB, BLK, columns), jnp.bfloat16)
        sent = jnp.concatenate([from_left[part], middle, from_right[part]], axis=0)
        out = own.astype(jnp.float32) + sent.astype(jnp.float32)
        for j in range(G):
            out = out + jnp.where(number == spots[j], hub_total[part, j][None], 0.0)
        return out.astype(jnp.bfloat16).reshape(tok_rows, columns)

    return (
        attended.reshape(tok_rows, columns),
        dq.reshape(tok_rows, columns),
        finish(dk, 0),
        finish(dv, 1),
    )


def solution(mesh):
    spec = P("ctx", "head")
    return jax.shard_map(
        local,
        mesh=mesh,
        in_specs=(spec, spec, spec, spec, P(), P()),
        out_specs=(spec, spec, spec, spec),
        check_vma=False,
    )
```

time: 718 us -> 223 us (0.31); the launches traced: 707 us -> 222 us
  local copies, waits for them, and re-layouts: 424 us -> 8.27 us
  matrix products: 183 us -> 0 us
  Pallas kernels: 0 us -> 73.4 us
  waiting for transfers between devices: 37.9 us -> 101 us
  other arithmetic: 35.4 us -> 10.6 us
    dot_general x34 -> x0, matrix products: 173 us -> none  [the longest x4 35.9 us: grad_group(): jnp.dot(spots.T, value_part.reshape(spots.shape[0], -1), precision=lax.Pr...]
    gather x24 -> x0, local copies, waits for them, and re-layouts: 150 us -> none  [the longest x16 104 us: block_scores(): gathered = key_store[entries]]
    reshape x12 -> x0, local copies, waits for them, and re-layouts: 87.7 us -> none  [the longest x4 36.2 us: grad_group(): value_part.reshape(spots.shape[0], -1)]
    transpose x8 -> x0, local copies, waits for them, and re-layouts: 79.3 us -> none  [the longest x4 39.6 us: grad_group(): jnp.einsum('bhqek,bqhd->bekhd', weights, pushed_rows, preferred_element_t...]
    pallas_call x0 -> x1, Pallas kernels: none -> 73.4 us  [attend(): pl.pallas_call(functools.partial(attend_kernel, total_blocks, local_lists...]
    scatter-add x2 -> x0, local copies, waits for them, and re-layouts: 33.9 us -> none  [the longest x1 20.5 us: local(): owned_rows = owned_rows.at[:HB].add(returned[:HB])]
    psum x2, waiting for transfers between devices: 36 us -> 68 us  [the longest x1 41.4 us: local(): hub = lax.psum(jnp.stack([pick(k), pick(v)]), 'ctx')]
    ppermute x4, waiting for transfers between devices: 1.87 us -> 32.5 us  [the longest x1 25.6 us: local(): from_left = lax.ppermute(dright, 'ctx', up)]
  transfers between devices with their start and end apart: 6 -> 6, of which waited for: 3 -> 4; matrix products, arithmetic and copies ran while one was open for 13% -> 4% of each run, Pallas kernels for 0% -> 0%
where the time goes in v1:
time: 223 us; the launch traced here: 222 us
  waiting for transfers between devices  101 us (45%)
  Pallas kernels  73.4 us (33%)
  between operations  18.1 us (8%)
  starting transfers between devices  11.2 us (5%)
  other arithmetic  10.6 us (5%)
  local copies, waits for them, and re-layouts  8.27 us (4%)
    pallas_call x1, Pallas kernels, attend(): pl.pallas_call(functools.partial(attend_kernel, total_blocks, local_lists...  73.4 us
    psum x1, waiting for transfers between devices, local(): hub = lax.psum(jnp.stack([pick(k), pick(v)]), 'ctx')  41.4 us
    psum x1, waiting for transfers between devices, local(): hub_total = lax.psum(dhub, 'ctx')  26.7 us
    ppermute x1, waiting for transfers between devices, local(): from_left = lax.ppermute(dright, 'ctx', up)  25.6 us
    ppermute x1, waiting for transfers between devices, local(): from_right = lax.ppermute(dleft, 'ctx', down)  6.93 us
    convert_element_type x1, other arithmetic, finish(): return out.astype(jnp.bfloat16).reshape(tok_rows, columns)  5.87 us
    ppermute x1, starting transfers between devices, local(): left = lax.ppermute(jnp.stack([k[-HB:], v[-HB:]]), 'ctx', up)  5.01 us
  transfers between devices with their start and end apart: 6, of which 4 were waited for; matrix products, arithmetic and copies ran while one was open for 4% of the time, Pallas kernels for 0%

profile of v1, /device:TPU:0, one launch (start us, length us, event | category | flops | bytes accessed | tf_op | source)
XLA Modules:
  0.0 222.1 jit_solution(4696191418585157965)
XLA Ops:
  7.2 0.0 all-reduce.3.cloned.1.call-start
  7.2 1.2 fusion
  8.4 0.0 copy-start.5
  8.4 1.2 fusion.1
  9.6 0.1 pad_maximum_fusion
  9.7 5.0 %collective-permute-start = (bf16[2,3,128,512]{3,2,1,0:T(8,128)(2,1)S(1)}, bf16[2,3,128,512]{3,2,1,0:T(8,128)(2,1)S(1)}, u32[]{:S(2)}, u32[]{:S(2)}) collective-permute-start(bf16[2,3,128,512]{3,2,1,0:T(8,128)(2,1)S(1)} %pad_maximum_fusion), channel_id=1, source_target_pairs={{0,8},{8,16},{16,24},{1,9},{9,17},{17,25},{2,10},{10,18},{18,26},{... | collective-permute-start | bytes 2359304 | tf_op jit(solution)/shard_map/ppermute | solution.py:196
  14.7 0.1 pad_maximum_fusion.1
  14.7 0.0 copy-start.4
  14.8 1.3 collective-permute-start.1
  16.1 0.0 copy-done.5
  16.1 0.6 fusion.4
  19.3 0.6 fusion.3
  21.2 2.4 %dynamic-slice_select_fusion.1 = (bf16[1,128,512]{2,1,0:T(8,128)(2,1)S(1)}, bf16[1,128,512]{2,1,0:T(8,128)(2,1)S(1)}, bf16[1,128,512]{2,1,0:T(8,128)(2,1)S(1)}, bf16[1,128,512]{2,1,0:T(8,128)(2,1)S(1)}) fusion(bf16[16,128,512]{2,1,0:T(8,128)(2,1)} %bitcast.40, s32[]{:T(128)S(6)} %select_n.49, pred[]{:T(512)} %bitcast.8, s32[]{:T(128)S(6)} %select_n.52, ...), kind=kLoop, calls=%fused_computation.16 | loop fusion | flops 262144 | bytes 1048586 | tf_op jit(solution)/shard_map/jit(_where)/select_n | solution.py:190
  23.7 0.8 pad_maximum_fusion.2
  24.5 0.0 all-reduce.3.cloned.1.call-update
  24.5 0.0 all-reduce.5.cloned.1.call-start
  24.6 0.0 copy-done.4
  24.6 0.7 copy.10.lists_ref
  25.3 41.4 %all-reduce.3.cloned.1.call-done.hub_ref = bf16[2,2,128,512]{3,2,1,0:T(8,128)(2,1)} async-done(((bf16[2,2,128,512]{3,2,1,0:T(8,128)(2,1)}), bf16[2,2,128,512]{3,2,1,0:T(8,128)(2,1)}) %all-reduce.3.cloned.1.call-update) | async-done | bytes 524304 | tf_op jit(solution)/shard_map/psum | solution.py:195
  66.6 0.0 collective-permute-done.left_ref
  66.6 0.0 copy-start.2
  66.6 0.0 collective-permute-done.1.right_ref
  66.7 0.0 copy-start.3
  66.7 0.9 copy-done.2
  67.5 0.3 copy-done.3
  67.8 73.4 %attend.1 = (bf16[16,128,512]{2,1,0:T(8,128)(2,1)}, bf16[16,128,512]{2,1,0:T(8,128)(2,1)}, bf16[16,128,512]{2,1,0:T(8,128)(2,1)}, bf16[16,128,512]{2,1,0:T(8,128...) custom-call(s32[64,6]{1,0:T(8,128)} %copy.10.lists_ref, ...), custom_call_target="tpu_custom_call" | custom-call | tf_op jit(solution)/shard_map/attend/pallas_call | solution.py:154
  141.2 3.5 %collective-permute-start.2 = (bf16[2,3,128,512]{3,2,1,0:T(8,128)(2,1)}, bf16[2,3,128,512]{3,2,1,0:T(8,128)(2,1)S(1)}, u32[]{:S(2)}, u32[]{:S(2)}) collective-permute-start(bf16[2,3,128,512]{3,2,1,0:T(8,128)(2,1)} %get-tuple-element.14), channel_id=1, source_target_pairs={{0,8},{8,16},{16,24},{1,9},{9,17},{17,25},{2,10},{10,18},{18,26},{... | collective-permute-start | bytes 2359304 | tf_op jit(solution)/shard_map/ppermute | solution.py:202
  144.7 0.0 all-reduce.5.cloned.1.call-update
  144.7 1.3 collective-permute-start.3
  146.0 0.1 pad.4.clone
  146.1 0.6 fusion.2
  146.7 1.3 iota_compare_fusion
  148.0 25.6 %collective-permute-done.2 = bf16[2,3,128,512]{3,2,1,0:T(8,128)(2,1)S(1)} collective-permute-done((bf16[2,3,128,512]{3,2,1,0:T(8,128)(2,1)}, bf16[2,3,128,512]{3,2,1,0:T(8,128)(2,1)S(1)}, u32[]{:S(2)}, u32[]{:S(2)}) %collective-permute-start.2) | collective-permute-done | bytes 786464 | tf_op jit(solution)/shard_map/ppermute | solution.py:202
  173.6 0.1 slice_bitcast_fusion.1
  173.6 0.0 copy-start
  173.7 6.9 %collective-permute-done.3 = bf16[2,3,128,512]{3,2,1,0:T(8,128)(2,1)S(1)} collective-permute-done((bf16[2,3,128,512]{3,2,1,0:T(8,128)(2,1)}, bf16[2,3,128,512]{3,2,1,0:T(8,128)(2,1)S(1)}, u32[]{:S(2)}, u32[]{:S(2)}) %collective-permute-start.3) | collective-permute-done | bytes 786464 | tf_op jit(solution)/shard_map/ppermute | solution.py:201
  180.6 0.8 slice_bitcast_fusion
  181.4 26.7 %all-reduce.5.cloned.1.call-done = f32[2,2,128,512]{3,2,1,0:T(8,128)} async-done(((f32[2,2,128,512]{3,2,1,0:T(8,128)}), f32[2,2,128,512]{3,2,1,0:T(8,128)}) %all-reduce.5.cloned.1.call-update) | async-done | bytes 1048592 | tf_op jit(solution)/shard_map/psum | solution.py:203
  208.1 0.0 copy-start.1
  208.1 1.3 slice_bitcast_fusion.5
  209.4 0.0 copy-done
  209.4 0.0 copy-done.1
  209.4 5.9 %add_convert_fusion = (bf16[16,128,512]{2,1,0:T(8,128)(2,1)}, bf16[16,128,512]{2,1,0:T(8,128)(2,1)}) fusion(bf16[16,128,512]{2,1,0:T(8,128)(2,1)} %get-tuple-element.17, bf16[3,128,512]{2,1,0:T(8,128)(2,1)S(1)} %get-tuple-element.34, bf16[3,128,512]{2,1,0:T(8,128)(2,1)S(1)} %get-tuple-element.32, f32[128,512]{1,0:T(8,128)S(1)} %get-tuple-element.29, ...), kind=kLoop, calls=%fused_computation | loop fusion | flops 20971520 | bytes 11010112 | tf_op jit(solution)/shard_map/convert_element_type | solution.py:212
  (5 shorter events, 0.1 us)
Async XLA Ops:
  7.2 59.5 %all-reduce.3.cloned.1.call-start = ((), (), s32[]{:S(2)}) async-start(), calls=%async_computation | async-start | bytes 1048576 | tf_op jit(solution)/shard_map/psum | solution.py:195
  8.4 7.7 %copy-start.5 = (s32[2]{0:T(128)S(1)}, s32[2]{0:T(128)}, u32[]{:S(2)}) copy-start(s32[2]{0:T(128)} %param.10) | copy-start | bytes 28
  9.7 57.0 %collective-permute-start = (bf16[2,3,128,512]{3,2,1,0:T(8,128)(2,1)S(1)}, bf16[2,3,128,512]{3,2,1,0:T(8,128)(2,1)S(1)}, u32[]{:S(2)}, u32[]{:S(2)}) collective-permute-start(bf16[2,3,128,512]{3,2,1,0:T(8,128)(2,1)S(1)} %pad_maximum_fusion), channel_id=1, source_target_pairs={{0,8},{8,16},{16,24},{1,9},{9,17},{17,25},{2,10},{10,18},{18,26},{... | collective-permute-start | bytes 2359304 | tf_op jit(solution)/shard_map/ppermute | solution.py:196
  14.7 9.8 %copy-start.4 = (s32[64,6]{0,1:T(8,128)S(1)}, s32[64,6]{0,1:T(8,128)}, u32[]{:S(2)}) copy-start(s32[64,6]{0,1:T(8,128)} %param.11) | copy-start | bytes 4612
  14.8 51.9 %collective-permute-start.1 = (bf16[2,3,128,512]{3,2,1,0:T(8,128)(2,1)S(1)}, bf16[2,3,128,512]{3,2,1,0:T(8,128)(2,1)S(1)}, u32[]{:S(2)}, u32[]{:S(2)}) collective-permute-start(bf16[2,3,128,512]{3,2,1,0:T(8,128)(2,1)S(1)} %pad_maximum_fusion.1), channel_id=1, source_target_pairs={{8,0},{16,8},{24,16},{9,1},{17,9},{25,17},{10,2},{18,10},{26,18},{... | collective-permute-start | bytes 2359304 | tf_op jit(solution)/shard_map/ppermute | solution.py:197
  24.5 183.6 %all-reduce.5.cloned.1.call-start = ((), (), s32[]{:S(2)}) async-start(), calls=%async_computation.1 | async-start | bytes 2097152 | tf_op jit(solution)/shard_map/psum | solution.py:203
  66.6 0.9 copy-start.2
  66.7 1.1 copy-start.3
  141.2 32.4 %collective-permute-start.2 = (bf16[2,3,128,512]{3,2,1,0:T(8,128)(2,1)}, bf16[2,3,128,512]{3,2,1,0:T(8,128)(2,1)S(1)}, u32[]{:S(2)}, u32[]{:S(2)}) collective-permute-start(bf16[2,3,128,512]{3,2,1,0:T(8,128)(2,1)} %get-tuple-element.14), channel_id=1, source_target_pairs={{0,8},{8,16},{16,24},{1,9},{9,17},{17,25},{2,10},{10,18},{18,26},{... | collective-permute-start | bytes 2359304 | tf_op jit(solution)/shard_map/ppermute | solution.py:202
  144.7 35.9 %collective-permute-start.3 = (bf16[2,3,128,512]{3,2,1,0:T(8,128)(2,1)}, bf16[2,3,128,512]{3,2,1,0:T(8,128)(2,1)S(1)}, u32[]{:S(2)}, u32[]{:S(2)}) collective-permute-start(bf16[2,3,128,512]{3,2,1,0:T(8,128)(2,1)} %get-tuple-element.15), channel_id=1, source_target_pairs={{8,0},{16,8},{24,16},{9,1},{17,9},{25,17},{10,2},{18,10},{26,18},{... | collective-permute-start | bytes 2359304 | tf_op jit(solution)/shard_map/ppermute | solution.py:201
  173.6 35.8 %copy-start = (bf16[16,128,512]{2,1,0:T(8,128)(2,1)S(1)}, bf16[16,128,512]{2,1,0:T(8,128)(2,1)}, u32[]{:S(2)}) copy-start(bf16[16,128,512]{2,1,0:T(8,128)(2,1)} %get-tuple-element.13) | copy-start | bytes 6291460
  208.1 1.3 copy-start.1
Sparse Core Ops, SparseCore 0:
  24.7 41.9 all-reduce.2
  144.8 63.2 all-reduce.4

commit v2 on v1

--- a/solution.py
+++ b/solution.py
@@ -16,10 +16,12 @@
 
 
 def attend_kernel(
-    total_blocks,
     listed,
     width,
-    lists_ref,
+    chained,
+    number_ref,
+    spots_ref,
+    bias_ref,
     q_ref,
     k_ref,
     v_ref,
@@ -27,27 +29,17 @@
     left_ref,
     right_ref,
     hub_ref,
-    att_ref,
-    dq_ref,
-    dk_ref,
-    dv_ref,
-    dleft_ref,
-    dright_ref,
-    dhub_ref,
-    kx,
-    vx,
-    kt,
-    vt,
-    dka,
-    dva,
+    *refs,
 ):
+    refs = refs[4:] if chained else refs
+    att_ref, dq_ref, dk_ref, dv_ref, dleft_ref, dright_ref, dhub_ref = refs[:7]
+    kx, vx, kt, vt, dka, dva = refs[7:]
     blocks = q_ref.shape[0]
     extended = blocks + 2 * HB
     store = extended + G
     heads = width // DH
     scale = 1.0 / math.sqrt(DH)
     c = scale * math.log2(math.e)
-    first_block = lax.axis_index("ctx") * blocks
 
     kx[0:HB] = left_ref[0]
     vx[0:HB] = left_ref[1]
@@ -69,18 +61,9 @@
 
     lax.fori_loop(0, store, flip, 0)
 
-    def body(b, carry):
-        spots = []
-        bias = []
-        for j in range(listed):
-            offset = lists_ref[first_block + b, j]
-            there = first_block + b + offset
-            alive = (there >= 0) & (there < total_blocks)
-            spots.append(HB + b + offset)
-            bias.append(jnp.where(alive, 0.0, DEAD))
-        for j in range(G):
-            spots.append(extended + j)
-            bias.append(0.0)
+    def block(b, kept):
+        spots = [HB + b + spots_ref[b, j] for j in range(kept)] + [extended + j for j in range(G)]
+        bias = [bias_ref[b, j] for j in range(kept)] + [0.0] * G
         n = len(spots)
         for h in range(heads):
             hs = slice(h * DH, (h + 1) * DH)
@@ -117,6 +100,14 @@
             for e in range(n):
                 dka[spots[e], h] += dk_part[e * BLK : (e + 1) * BLK]
                 dva[spots[e], h] += dv_part[e * BLK : (e + 1) * BLK]
+
+    sizes = [min(4, listed)] + list(range(5, listed + 1))
+
+    def body(b, carry):
+        kept = number_ref[b]
+        for at, size in enumerate(sizes):
+            fits = kept <= size if at == 0 else kept == size
+            pl.when(fits)(functools.partial(block, b, size))
         return carry
 
     lax.fori_loop(0, blocks, body, 0)
@@ -140,23 +131,168 @@
     lax.fori_loop(0, blocks, finish, 0)
 
 
-def attend(local_lists, q, k, v, g, left, right, hub, total_blocks):
+def chain_kernel(x_ref, out_ref, from_left, from_right, to_right, to_left, sends, recvs):
+    me = lax.axis_index("ctx")
+    count = lax.axis_size("ctx")
+    last = count - 1
+    chunks = x_ref.shape[0]
+    mesh_ids = pl.DeviceIdType.MESH
+
+    barrier = pltpu.get_barrier_semaphore()
+
+    @pl.when(me > 0)
+    def _():
+        pl.semaphore_signal(barrier, inc=1, device_id={"ctx": me - 1}, device_id_type=mesh_ids)
+
+    @pl.when(me < last)
+    def _():
+        pl.semaphore_signal(barrier, inc=1, device_id={"ctx": me + 1}, device_id_type=mesh_ids)
+
+    @pl.when((me > 0) & (me < last))
+    def _():
+        pl.semaphore_wait(barrier, 2)
+
+    @pl.when((me == 0) | (me == last))
+    def _():
+        pl.semaphore_wait(barrier, 1)
+
+    def rightward(source, i):
+        return pltpu.make_async_remote_copy(
+            src_ref=source.at[i],
+            dst_ref=from_left.at[i],
+            send_sem=sends.at[0, i],
+            recv_sem=recvs.at[0, i],
+            device_id={"ctx": me + 1},
+            device_id_type=mesh_ids,
+        )
+
+    def leftward(source, i):
+        return pltpu.make_async_remote_copy(
+            src_ref=source.at[i],
+            dst_ref=from_right.at[i],
+            send_sem=sends.at[1, i],
+            recv_sem=recvs.at[1, i],
+            device_id={"ctx": me - 1},
+            device_id_type=mesh_ids,
+        )
+
+    def step(s, carry):
+        i = s - me
+
+        @pl.when((i >= 0) & (i < chunks))
+        def _():
+            @pl.when(me == 0)
+            def _():
+                rightward(x_ref, i).start()
+
+            @pl.when(me > 0)
+            def _():
+                rightward(to_right, i).wait_recv()
+
+            @pl.when((me > 0) & (me < last))
+            def _():
+                to_right[i] = x_ref[i] + from_left[i]
+                rightward(to_right, i).start()
+
+        j = s - (last - me)
+
+        @pl.when((j >= 0) & (j < chunks))
+        def _():
+            @pl.when(me == last)
+            def _():
+                leftward(x_ref, j).start()
+
+            @pl.when(me < last)
+            def _():
+                leftward(to_left, j).wait_recv()
+
+            @pl.when((me > 0) & (me < last))
+            def _():
+                to_left[j] = x_ref[j] + from_right[j]
+                leftward(to_left, j).start()
+
+        return carry
+
+    lax.fori_loop(0, chunks + last, step, 0)
+
+    def close(i, carry):
+        own = x_ref[i].astype(jnp.float32)
+
+        @pl.when(me == 0)
+        def _():
+            out_ref[i] = (own + from_right[i].astype(jnp.float32)).astype(out_ref.dtype)
+
+        @pl.when(me == last)
+        def _():
+            out_ref[i] = (own + from_left[i].astype(jnp.float32)).astype(out_ref.dtype)
+
+        @pl.when((me > 0) & (me < last))
+        def _():
+            both = from_left[i].astype(jnp.float32) + from_right[i].astype(jnp.float32)
+            out_ref[i] = (own + both).astype(out_ref.dtype)
+
+        @pl.when(me < last)
+        def _():
+            rightward(to_right, i).wait_send()
+
+        @pl.when(me > 0)
+        def _():
+            leftward(to_left, i).wait_send()
+
+        return carry
+
+    lax.fori_loop(0, chunks, close, 0)
+
+
+def chain_sum(a, ident):
+    columns = a.shape[-1]
+    pieces = 8
+    rows = a.size // columns // pieces
+    flat = a.reshape(pieces, rows, columns)
+    buffer = pltpu.VMEM(flat.shape, flat.dtype)
+    out = pl.pallas_call(
+        chain_kernel,
+        out_shape=jax.ShapeDtypeStruct(flat.shape, flat.dtype),
+        in_specs=[pl.BlockSpec(memory_space=pltpu.VMEM)],
+        out_specs=pl.BlockSpec(memory_space=pltpu.VMEM),
+        scratch_shapes=[buffer] * 4
+        + [pltpu.SemaphoreType.DMA((2, pieces)), pltpu.SemaphoreType.DMA((2, pieces))],
+        compiler_params=pltpu.CompilerParams(
+            collective_id=ident, has_side_effects=True, vmem_limit_bytes=16 << 20
+        ),
+        cost_estimate=pl.CostEstimate(
+            flops=4 * a.size, bytes_accessed=120 * a.size, transcendentals=0
+        ),
+        name=f"chain{ident}",
+    )(flat)
+    return out.reshape(a.shape)
+
+
+def attend(base, width, table, q, k, v, g, left, right, hub, earlier):
     blocks, _, columns = q.shape
-    width = 2 * DH if columns % (2 * DH) == 0 else DH
     heads = width // DH
+    number, offsets, bias = table
+    listed = offsets.shape[1]
     store = blocks + 2 * HB + G
-    whole = pl.BlockSpec((blocks, BLK, width), lambda i: (0, 0, i))
-    rim = pl.BlockSpec((2, HB, BLK, width), lambda i: (0, 0, 0, i))
-    hubs = pl.BlockSpec((2, G, BLK, width), lambda i: (0, 0, 0, i))
+    whole = pl.BlockSpec((blocks, BLK, width), lambda i: (0, 0, base))
+    rim = pl.BlockSpec((2, HB, BLK, width), lambda i: (0, 0, 0, 0))
+    hubs_in = pl.BlockSpec((2, G, BLK, width), lambda i: (0, 0, 0, base))
+    hubs = pl.BlockSpec((2, G, BLK, width), lambda i: (0, 0, 0, 0))
     big = jax.ShapeDtypeStruct(q.shape, jnp.bfloat16)
     rim_shape = jax.ShapeDtypeStruct(left.shape, jnp.bfloat16)
-    hub_shape = jax.ShapeDtypeStruct(hub.shape, jnp.float32)
+    hub_shape = jax.ShapeDtypeStruct((2, G, BLK, width), jnp.bfloat16)
+    smem = pl.BlockSpec(memory_space=pltpu.SMEM)
+    units = 6 * heads * blocks * (listed + G)
     return pl.pallas_call(
-        functools.partial(attend_kernel, total_blocks, local_lists.shape[1], width),
-        grid=(columns // width,),
-        in_specs=[pl.BlockSpec(memory_space=pltpu.SMEM)] + [whole] * 4 + [rim, rim, hubs],
+        functools.partial(attend_kernel, listed, width, bool(earlier)),
+        grid=(1,),
+        in_specs=[smem] * 3
+        + [whole] * 4
+        + [rim, rim, hubs_in]
+        + [pl.BlockSpec(memory_space=pl.ANY)] * len(earlier),
         out_specs=[whole] * 4 + [rim, rim, hubs],
         out_shape=[big] * 4 + [rim_shape, rim_shape, hub_shape],
+        input_output_aliases={10 + i: i for i in range(len(earlier))},
         scratch_shapes=[
             pltpu.VMEM((store, BLK, width), jnp.bfloat16),
             pltpu.VMEM((store, BLK, width), jnp.bfloat16),
@@ -165,9 +301,34 @@
             pltpu.VMEM((store, heads, BLK, DH), jnp.float32),
             pltpu.VMEM((store, heads, BLK, DH), jnp.float32),
         ],
-        compiler_params=pltpu.CompilerParams(vmem_limit_bytes=60 << 20),
+        compiler_params=pltpu.CompilerParams(vmem_limit_bytes=56 << 20),
+        cost_estimate=pl.CostEstimate(
+            flops=8 * units * 2 * BLK * BLK * DH,
+            bytes_accessed=16 * blocks * BLK * width,
+            transcendentals=heads * blocks * (listed + G) * BLK * BLK,
+        ),
         name="attend",
-    )(local_lists, q, k, v, g, left, right, hub)
+    )(number, offsets, bias, q, k, v, g, left, right, hub, *earlier)
+
+
+def entry_table(local_lists, first_block, blocks, total_blocks):
+    lists = lax.dynamic_slice_in_dim(local_lists, first_block, blocks, 0)
+    listed = lists.shape[1]
+    reach = jnp.arange(-HB, HB + 1, dtype=jnp.int32)
+    there = first_block + jnp.arange(blocks, dtype=jnp.int32)[:, None] + reach[None, :]
+    alive = (there >= 0) & (there < total_blocks)
+    times = jnp.sum(lists[:, :, None] == reach[None, None, :], axis=1).astype(jnp.int32)
+    times = jnp.where(alive, times, 0)
+    kept = times > 0
+    before = (reach[None, :] < reach[:, None]).astype(jnp.int32)
+    rank = jnp.sum(kept.astype(jnp.int32)[:, None, :] * before[None], axis=2)
+    seat = kept[:, None, :] & (rank[:, None, :] == jnp.arange(listed)[None, :, None])
+    offsets = jnp.sum(jnp.where(seat, reach[None, None, :], 0), axis=2).astype(jnp.int32)
+    seat_times = jnp.sum(jnp.where(seat, times[:, None, :], 0), axis=2)
+    bias = jnp.where(
+        seat_times > 0, jnp.log2(jnp.maximum(seat_times, 1).astype(jnp.float32)), DEAD
+    ).astype(jnp.float32)
+    return jnp.sum(kept.astype(jnp.int32), axis=1), offsets, bias
 
 
 def local(query_rows, key_rows, value_rows, out_grad, hub_blocks, local_lists):
@@ -185,22 +346,49 @@
     here = (spots >= 0) & (spots < blocks)
     clipped = jnp.clip(spots, 0, blocks - 1)
 
+    table = entry_table(local_lists, first_block, blocks, total_blocks)
+    width = 2 * DH if columns % (2 * DH) == 0 else DH
+
     def pick(a):
         rows = [
-            jnp.where(here[j], lax.dynamic_index_in_dim(a, clipped[j], 0, keepdims=False), 0)
+            jnp.where(here[j], lax.dynamic_slice_in_dim(a, clipped[j], 1, 0), 0)
             for j in range(G)
         ]
-        return jnp.stack(rows)
-
-    hub = lax.psum(jnp.stack([pick(k), pick(v)]), "ctx")
-    left = lax.ppermute(jnp.stack([k[-HB:], v[-HB:]]), "ctx", up)
-    right = lax.ppermute(jnp.stack([k[:HB], v[:HB]]), "ctx", down)
-    attended, dq, dk, dv, dleft, dright, dhub = attend(
-        local_lists, q, k, v, g, left, right, hub, total_blocks
+        return jnp.concatenate(rows, axis=0)
+
+    def rims(base):
+        own = slice(base * width, (base + 1) * width)
+        low = jnp.stack([k[:HB, :, own], v[:HB, :, own]])
+        high = jnp.stack([k[blocks - HB :, :, own], v[blocks - HB :, :, own]])
+        return low, high
+
+    def shifted(low, high):
+        return lax.ppermute(high, "ctx", up), lax.ppermute(low, "ctx", down)
+
+    earlier = ()
+    returned = []
+    hub_grads = []
+    groups = columns // width
+    arrived = shifted(*rims(0))
+    hub = chain_sum(jnp.stack([pick(k), pick(v)]), 1)
+    for base in range(groups):
+        coming = None
+        if base + 1 < groups:
+            ahead, arrived, hub = lax.optimization_barrier((rims(base + 1), arrived, hub))
+            coming = shifted(*ahead)
+        done = attend(base, width, table, q, k, v, g, *arrived, hub, earlier)
+        arrived = coming
+        earlier = done[:4]
+        dleft, dright, dhub = done[4:]
+        returned.append((lax.ppermute(dright, "ctx", up), lax.ppermute(dleft, "ctx", down)))
+        hub_grads.append(dhub)
+    dhub = jnp.concatenate(hub_grads, axis=3) if groups > 1 else hub_grads[0]
+    hub_total = chain_sum(dhub, 2)
+    attended, dq, dk, dv = earlier
+    from_left, from_right = (
+        jnp.concatenate(pieces, axis=3) if len(pieces) > 1 else pieces[0]
+        for pieces in zip(*returned)
     )
-    from_right = lax.ppermute(dleft, "ctx", down)
-    from_left = lax.ppermute(dright, "ctx", up)
-    hub_total = lax.psum(dhub, "ctx")
     number = jnp.arange(blocks, dtype=jnp.int32)[:, None, None]
 
     def finish(own, part):
@@ -208,7 +396,8 @@
         sent = jnp.concatenate([from_left[part], middle, from_right[part]], axis=0)
         out = own.astype(jnp.float32) + sent.astype(jnp.float32)
         for j in range(G):
-            out = out + jnp.where(number == spots[j], hub_total[part, j][None], 0.0)
+            chosen = hub_total[part, j][None].astype(jnp.float32)
+            out = out + jnp.where(number == spots[j], chosen, 0.0)
         return out.astype(jnp.bfloat16).reshape(tok_rows, columns)
 
     return (

time: 223 us -> 193 us (0.87)
  waiting for transfers between devices: 101 us -> 0.02 us
  Pallas kernels: 73.4 us -> 144 us
  between operations: 18.1 us -> 4.92 us
  starting transfers between devices: 11.2 us -> 23.4 us
    pallas_call x1 -> x4, Pallas kernels: 73.4 us -> 144 us  [the longest x2 72 us: chain_sum(): pl.pallas_call(chain_kernel, out_shape=jax.ShapeDtypeStruct(flat.shape, f...]
    psum x2 -> x0, waiting for transfers between devices: 68 us -> none  [the longest x1 41.4 us: local(): hub = lax.psum(jnp.stack([pick(k), pick(v)]), 'ctx')]
    ppermute x4 -> x8, waiting for transfers between devices: 32.5 us -> 0.02 us  [the longest x4 0.01 us: shifted(): return (lax.ppermute(high, 'ctx', up), lax.ppermute(low, 'ctx', down))]
    ppermute x4 -> x8, starting transfers between devices: 11.1 us -> 23.4 us  [the longest x2 11.8 us: local(): lax.ppermute(dright, 'ctx', up)]
    another operation x1 -> x3, local copies, waits for them, and re-layouts: 0.01 us -> 2.56 us  [the longest x2 2.56 us: rims(): low = jnp.stack([k[:HB, :, own], v[:HB, :, own]])]
    slice x3 -> x1, local copies, waits for them, and re-layouts: 2.95 us -> 0.6 us  [finish(): out = out + jnp.where(number == spots[j], chosen, 0.0)]
  transfers between devices with their start and end apart: 6 -> 8, of which waited for: 4 -> 0; matrix products, arithmetic and copies ran while one was open for 4% -> 5% of each run, Pallas kernels for 0% -> 75%
where the time goes in v2:
time: 193 us; the launch traced here: 192 us
  Pallas kernels  144 us (75%)
  starting transfers between devices  23.4 us (12%)
  other arithmetic  11.1 us (6%)
  local copies, waits for them, and re-layouts  9.13 us (5%)
  between operations  4.92 us (3%)
    pallas_call x2, Pallas kernels, chain_sum(): pl.pallas_call(chain_kernel, out_shape=jax.ShapeDtypeStruct(flat.shape, f...  72 us
    pallas_call x2, Pallas kernels, attend(): pl.pallas_call(functools.partial(attend_kernel, listed, width, bool(earli...  71.9 us
    ppermute x2, starting transfers between devices, local(): lax.ppermute(dright, 'ctx', up)  11.8 us
    ppermute x4, starting transfers between devices, shifted(): return (lax.ppermute(high, 'ctx', up), lax.ppermute(low, 'ctx', down))  8.89 us
    convert_element_type x1, other arithmetic, finish(): return out.astype(jnp.bfloat16).reshape(tok_rows, columns)  4.61 us
  transfers between devices with their start and end apart: 8, of which 0 were waited for; matrix products, arithmetic and copies ran while one was open for 5% of the time, Pallas kernels for 75%

profile of v2, /device:TPU:0, one launch (start us, length us, event | category | flops | bytes accessed | tf_op | source)
XLA Modules:
  0.0 192.5 jit_solution(13923385348635317862)
XLA Ops:
  0.6 0.0 copy-start
  0.6 0.0 copy-start.5
  0.7 1.3 slice_bitcast_fusion.5
  1.9 1.3 slice_bitcast_fusion.4
  3.3 5.0 %collective-permute-start = (bf16[2,3,128,256]{3,2,1,0:T(8,128)(2,1)S(1)}, bf16[2,3,128,256]{3,2,1,0:T(8,128)(2,1)S(1)}, u32[]{:S(2)}, u32[]{:S(2)}) collective-permute-start(bf16[2,3,128,256]{3,2,1,0:T(8,128)(2,1)S(1)} %pad_maximum_fusion.4), channel_id=1, source_target_pairs={{0,8},{8,16},{16,24},{1,9},{9,17},{17,25},{2,10},{10,18},{18,26},{... | collective-permute-start | bytes 1179656 | tf_op jit(solution)/shard_map/ppermute | solution.py:366
  8.3 1.3 collective-permute-start.1
  9.6 0.0 copy-done.5
  9.6 0.6 fusion.11
  12.8 0.6 fusion.9
  13.4 0.6 fusion.10
  14.0 0.1 compare_convert_fusion
  14.1 0.0 copy-done
  14.1 0.1 constant_dynamic-slice_fusion
  14.2 0.1 convert_reduce_fusion
  14.2 0.1 fusion.7
  14.3 0.5 convert_reduce_fusion.1.number_ref
  16.2 2.4 %dynamic-slice_select_fusion.1 = (bf16[1,128,512]{2,1,0:T(8,128)(2,1)S(1)}, bf16[1,128,512]{2,1,0:T(8,128)(2,1)S(1)}, bf16[1,128,512]{2,1,0:T(8,128)(2,1)S(1)}, bf16[1,128,512]{2,1,0:T(8,128)(2,1)S(1)}) fusion(bf16[16,128,512]{2,1,0:T(8,128)(2,1)} %bitcast.78, s32[]{:T(128)S(6)} %select_n.78, pred[]{:T(512)} %bitcast.12, s32[]{:T(128)S(6)} %select_n.81, ...), kind=kLoop, calls=%fused_computation.31 | loop fusion | flops 262144 | bytes 1048586 | tf_op jit(solution)/shard_map/jit(_where)/select_n | solution.py:354
  18.7 0.1 pad_maximum_fusion
  18.7 0.1 multiply_reduce_fusion
  18.8 0.1 select_reduce_fusion
  18.9 1.2 iota_compare_fusion.1
  20.1 0.1 copy.15
  20.2 0.7 copy.18.spots_ref
  20.9 0.1 pad.6.clone
  20.9 34.1 %chain1.1 = bf16[8,64,512]{2,1,0:T(8,128)(2,1)S(1)} custom-call(bf16[8,64,512]{2,1,0:T(8,128)(2,1)S(1)} %bitcast.67), custom_call_target="tpu_custom_call" | custom-call | flops 1048576 | bytes 31457280 | tf_op jit(solution)/shard_map/chain1/pallas_call | solution.py:253
  55.0 0.0 copy-start.1
  55.0 0.8 copy-done.1
  55.8 0.1 pad_maximum_fusion.2
  55.9 0.6 multiply_select_fusion.bias_ref
  56.5 0.0 collective-permute-done.left_ref
  56.5 0.0 copy-start.6
  56.5 0.0 collective-permute-done.1.right_ref
  56.5 0.0 copy-start.7
  56.5 1.3 collective-permute-start.2
  57.8 1.3 collective-permute-start.3
  59.1 0.0 copy-done.6
  59.1 0.0 copy-done.7
  59.1 35.9 %attend.2 = (bf16[16,128,512]{2,1,0:T(8,128)(2,1)}, bf16[16,128,512]{2,1,0:T(8,128)(2,1)}, bf16[16,128,512]{2,1,0:T(8,128)(2,1)}, bf16[16,128,512]{2,1,0:T(8,128...) custom-call(s32[16]{0:T(128)} %convert_reduce_fusion.1.number_ref, ...), custom_call_target="tpu_custom_call" | custom-call | flops 51539607552 | bytes 8388608 | tf_op jit(solution)/shard_map/attend/pallas_call | solution.py:286
  95.1 6.4 %collective-permute-start.4 = (bf16[2,3,128,256]{3,2,1,0:T(8,128)(2,1)}, bf16[2,3,128,256]{3,2,1,0:T(8,128)(2,1)S(1)}, u32[]{:S(2)}, u32[]{:S(2)}) collective-permute-start(bf16[2,3,128,256]{3,2,1,0:T(8,128)(2,1)} %get-tuple-element.35), channel_id=1, source_target_pairs={{0,8},{8,16},{16,24},{1,9},{9,17},{17,25},{2,10},{10,18},{18,26},{... | collective-permute-start | bytes 1179656 | tf_op jit(solution)/shard_map/ppermute | solution.py:383
  101.5 1.5 collective-permute-start.6
  103.0 0.0 collective-permute-done.2.left_ref
  103.0 0.0 copy-start.8
  103.0 0.0 collective-permute-done.3.right_ref
  103.0 0.0 copy-start.9
  103.0 0.7 copy-done.8
  103.8 0.1 copy-done.9
  103.9 35.9 %attend.3 = (bf16[16,128,512]{2,1,0:T(8,128)(2,1)}, bf16[16,128,512]{2,1,0:T(8,128)(2,1)}, bf16[16,128,512]{2,1,0:T(8,128)(2,1)}, bf16[16,128,512]{2,1,0:T(8,128...) custom-call(s32[16]{0:T(128)} %convert_reduce_fusion.1.number_ref, ...), custom_call_target="tpu_custom_call", output_to_operand_aliasing={{0}: (10, {}), {1}: (11, {}), {2}: (12, {}), {3}: (13, {})} | custom-call | flops 51539607552 | bytes 8388608 | tf_op jit(solution)/shard_map/attend/pallas_call | solution.py:286
  139.8 5.3 %collective-permute-start.5 = (bf16[2,3,128,256]{3,2,1,0:T(8,128)(2,1)}, bf16[2,3,128,256]{3,2,1,0:T(8,128)(2,1)S(1)}, u32[]{:S(2)}, u32[]{:S(2)}) collective-permute-start(bf16[2,3,128,256]{3,2,1,0:T(8,128)(2,1)} %get-tuple-element.36), channel_id=1, source_target_pairs={{0,8},{8,16},{16,24},{1,9},{9,17},{17,25},{2,10},{10,18},{18,26},{... | collective-permute-start | bytes 1179656 | tf_op jit(solution)/shard_map/ppermute | solution.py:383
  145.2 1.3 collective-permute-start.7
  146.5 0.0 copy-done.4
  146.5 1.0 pad_maximum_fusion.1
  147.5 0.0 collective-permute-done.4
  147.5 37.9 %chain2.1 = bf16[8,64,512]{2,1,0:T(8,128)(2,1)S(1)} custom-call(bf16[8,64,512]{2,1,0:T(8,128)(2,1)S(1)} %bitcast.68), custom_call_target="tpu_custom_call" | custom-call | flops 1048576 | bytes 31457280 | tf_op jit(solution)/shard_map/chain2/pallas_call | solution.py:253
  185.4 0.1 fusion.1
  185.6 0.0 collective-permute-done.6
  185.6 0.0 collective-permute-done.5
  185.6 0.0 copy-start.3
  185.7 0.0 copy-start.2
  185.7 0.1 slice_bitcast_fusion.1
  185.7 0.0 collective-permute-done.7
  185.8 0.1 slice_bitcast_fusion
  185.8 1.4 copy-done.3
  187.2 0.6 copy-done.2
  187.8 4.6 %add_convert_fusion = (bf16[16,128,512]{2,1,0:T(8,128)(2,1)}, bf16[16,128,512]{2,1,0:T(8,128)(2,1)}) fusion(bf16[16,128,512]{2,1,0:T(8,128)(2,1)S(1)} %copy-done.3, bf16[3,128,512]{2,1,0:T(8,128)(2,1)S(1)} %get-tuple-element.63, bf16[3,128,512]{2,1,0:T(8,128)(2,1)S(1)} %get-tuple-element.61, f32[128,512]{1,0:T(8,128)S(1)} %get-tuple-element.66, ...), kind=kLoop, calls=%fused_computation | loop fusion | flops 20971520 | bytes 11010112 | tf_op jit(solution)/shard_map/convert_element_type | solution.py:401
  (14 shorter events, 0.3 us)
Async XLA Ops:
  0.6 13.5 %copy-start = (s32[64,6]{0,1:T(8,128)S(1)}, s32[64,6]{0,1:T(8,128)}, u32[]{:S(2)}) copy-start(s32[64,6]{0,1:T(8,128)} %param.11) | copy-start | bytes 4612
  0.6 9.0 %copy-start.5 = (s32[2]{0:T(128)S(1)}, s32[2]{0:T(128)}, u32[]{:S(2)}) copy-start(s32[2]{0:T(128)} %param.10) | copy-start | bytes 28
  3.3 53.2 %collective-permute-start = (bf16[2,3,128,256]{3,2,1,0:T(8,128)(2,1)S(1)}, bf16[2,3,128,256]{3,2,1,0:T(8,128)(2,1)S(1)}, u32[]{:S(2)}, u32[]{:S(2)}) collective-permute-start(bf16[2,3,128,256]{3,2,1,0:T(8,128)(2,1)S(1)} %pad_maximum_fusion.4), channel_id=1, source_target_pairs={{0,8},{8,16},{16,24},{1,9},{9,17},{17,25},{2,10},{10,18},{18,26},{... | collective-permute-start | bytes 1179656 | tf_op jit(solution)/shard_map/ppermute | solution.py:366
  8.3 48.2 %collective-permute-start.1 = (bf16[2,3,128,256]{3,2,1,0:T(8,128)(2,1)S(1)}, bf16[2,3,128,256]{3,2,1,0:T(8,128)(2,1)S(1)}, u32[]{:S(2)}, u32[]{:S(2)}) collective-permute-start(bf16[2,3,128,256]{3,2,1,0:T(8,128)(2,1)S(1)} %pad_maximum_fusion.5), channel_id=1, source_target_pairs={{8,0},{16,8},{24,16},{9,1},{17,9},{25,17},{10,2},{18,10},{26,18},{... | collective-permute-start | bytes 1179656 | tf_op jit(solution)/shard_map/ppermute | solution.py:366
  55.0 0.8 copy-start.1
  56.5 2.6 %copy-start.6 = (bf16[2,3,128,256]{3,2,1,0:T(8,128)(2,1)}, bf16[2,3,128,256]{3,2,1,0:T(8,128)(2,1)S(1)}, u32[]{:S(2)}) copy-start(bf16[2,3,128,256]{3,2,1,0:T(8,128)(2,1)S(1)} %collective-permute-done.left_ref) | copy-start | bytes 1179652
  56.5 2.7 %copy-start.7 = (bf16[2,3,128,256]{3,2,1,0:T(8,128)(2,1)}, bf16[2,3,128,256]{3,2,1,0:T(8,128)(2,1)S(1)}, u32[]{:S(2)}) copy-start(bf16[2,3,128,256]{3,2,1,0:T(8,128)(2,1)S(1)} %collective-permute-done.1.right_ref) | copy-start | bytes 1179652
  56.5 46.5 %collective-permute-start.2 = (bf16[2,3,128,256]{3,2,1,0:T(8,128)(2,1)S(1)}, bf16[2,3,128,256]{3,2,1,0:T(8,128)(2,1)S(1)}, u32[]{:S(2)}, u32[]{:S(2)}) collective-permute-start(bf16[2,3,128,256]{3,2,1,0:T(8,128)(2,1)S(1)} %get-tuple-element.23), channel_id=1, source_target_pairs={{0,8},{8,16},{16,24},{1,9},{9,17},{17,25},{2,10},{10,18},{18,26},{... | collective-permute-start | bytes 1179656 | tf_op jit(solution)/shard_map/ppermute | solution.py:366
  57.8 45.2 %collective-permute-start.3 = (bf16[2,3,128,256]{3,2,1,0:T(8,128)(2,1)S(1)}, bf16[2,3,128,256]{3,2,1,0:T(8,128)(2,1)S(1)}, u32[]{:S(2)}, u32[]{:S(2)}) collective-permute-start(bf16[2,3,128,256]{3,2,1,0:T(8,128)(2,1)S(1)} %get-tuple-element.24), channel_id=1, source_target_pairs={{8,0},{16,8},{24,16},{9,1},{17,9},{25,17},{10,2},{18,10},{26,18},{... | collective-permute-start | bytes 1179656 | tf_op jit(solution)/shard_map/ppermute | solution.py:366
  95.1 52.4 %collective-permute-start.4 = (bf16[2,3,128,256]{3,2,1,0:T(8,128)(2,1)}, bf16[2,3,128,256]{3,2,1,0:T(8,128)(2,1)S(1)}, u32[]{:S(2)}, u32[]{:S(2)}) collective-permute-start(bf16[2,3,128,256]{3,2,1,0:T(8,128)(2,1)} %get-tuple-element.35), channel_id=1, source_target_pairs={{0,8},{8,16},{16,24},{1,9},{9,17},{17,25},{2,10},{10,18},{18,26},{... | collective-permute-start | bytes 1179656 | tf_op jit(solution)/shard_map/ppermute | solution.py:383
  101.5 84.0 %collective-permute-start.6 = (bf16[2,3,128,256]{3,2,1,0:T(8,128)(2,1)}, bf16[2,3,128,256]{3,2,1,0:T(8,128)(2,1)S(1)}, u32[]{:S(2)}, u32[]{:S(2)}) collective-permute-start(bf16[2,3,128,256]{3,2,1,0:T(8,128)(2,1)} %get-tuple-element.37), channel_id=1, source_target_pairs={{8,0},{16,8},{24,16},{9,1},{17,9},{25,17},{10,2},{18,10},{26,18},{... | collective-permute-start | bytes 1179656 | tf_op jit(solution)/shard_map/ppermute | solution.py:383
  103.0 0.8 copy-start.8
  103.0 0.9 copy-start.9
  103.9 42.6 %copy-start.4 = (bf16[2,2,128,256]{3,2,1,0:T(8,128)(2,1)S(1)}, bf16[2,2,128,256]{3,2,1,0:T(8,128)(2,1)}, u32[]{:S(2)}) copy-start(bf16[2,2,128,256]{3,2,1,0:T(8,128)(2,1)} %get-tuple-element.39) | copy-start | bytes 786436
  139.8 45.8 %collective-permute-start.5 = (bf16[2,3,128,256]{3,2,1,0:T(8,128)(2,1)}, bf16[2,3,128,256]{3,2,1,0:T(8,128)(2,1)S(1)}, u32[]{:S(2)}, u32[]{:S(2)}) collective-permute-start(bf16[2,3,128,256]{3,2,1,0:T(8,128)(2,1)} %get-tuple-element.36), channel_id=1, source_target_pairs={{0,8},{8,16},{16,24},{1,9},{9,17},{17,25},{2,10},{10,18},{18,26},{... | collective-permute-start | bytes 1179656 | tf_op jit(solution)/shard_map/ppermute | solution.py:383
  145.2 40.6 %collective-permute-start.7 = (bf16[2,3,128,256]{3,2,1,0:T(8,128)(2,1)}, bf16[2,3,128,256]{3,2,1,0:T(8,128)(2,1)S(1)}, u32[]{:S(2)}, u32[]{:S(2)}) collective-permute-start(bf16[2,3,128,256]{3,2,1,0:T(8,128)(2,1)} %get-tuple-element.38), channel_id=1, source_target_pairs={{8,0},{16,8},{24,16},{9,1},{17,9},{25,17},{10,2},{18,10},{26,18},{... | collective-permute-start | bytes 1179656 | tf_op jit(solution)/shard_map/ppermute | solution.py:383
  185.6 1.6 copy-start.3
  185.7 2.2 %copy-start.2 = (bf16[16,128,512]{2,1,0:T(8,128)(2,1)S(1)}, bf16[16,128,512]{2,1,0:T(8,128)(2,1)}, u32[]{:S(2)}) copy-start(bf16[16,128,512]{2,1,0:T(8,128)(2,1)} %get-tuple-element.34) | copy-start | bytes 6291460
